TPU v7x, 512 devices: a whole 4x4x16 slice. The times are simulated.
512 devices in a mesh: dp: 2 (over z_hi), fsdp: 16 (over z_lo, core), tile: 16 (over y, x).
Axes of the slice: x: 4, y: 4, z: 16 (z_hi: 2, z_lo: 8; z = z_hi * 8 + z_lo), core: 2. Of those that a mesh axis runs over, the one named last changes fastest.
Arguments:
- tokens: bfloat16 [32, 8, 512, 1536], P(('dp', 'fsdp'), None, 'tile'), may hold values from -6 to 6
- norm_gain: float32 [1536], replicated, may hold values from 0.25 to 1.75
- query_key_value_weight: bfloat16 [1536, 2304], P('fsdp'), may hold values from -5 to 5
- out_weight: bfloat16 [768, 1536], P('fsdp'), may hold values from -0.21875 to 0.21875
- head_weight: bfloat16 [1536, 320], P('fsdp'), may hold values from -0.15625 to 0.15625
- coarse: float32 [32, 20, 8, 512], P(('dp', 'fsdp'), None, None, 'tile'), may hold values from -36 to 36
- grad_fine: float32 [32, 20, 32, 2048], P(('dp', 'fsdp'), None, None, 'tile'), may hold values from -0.6 to 0.6
Outputs:
- fine_grid: float32 [32, 20, 32, 2048], P(('dp', 'fsdp'), None, None, 'tile')
- grad_tokens: bfloat16 [32, 8, 512, 1536], P(('dp', 'fsdp'), None, 'tile')
- grad_head: float32 [1536, 320], P('fsdp')
All inputs are finite; a program needn't handle non-finite values.
Results may differ from a plain program's by a relative error of at most 0.0059.
Values may be sent and summed in bfloat16 or wider, within the bound.
No kernel may reach another device: no remote copies, remote signals or barrier semaphores. Data moves between devices by JAX's collectives and lax.ppermute only.
A program may use at most 64 MiB of HBM per device.

v0:
```python
import jax
import jax.numpy as jnp
from jax import lax
from jax.sharding import PartitionSpec as P

D = 1536
HEADS = 8
HEAD_DIM = 96
VARS = 20
MARGIN = 8
INNER = 768
HEAD_OUT = 320
EPSILON = 1e-05


def with_halo(shard, sides, width):
    for axis, dim in sides:
        devices, length = (lax.axis_size(axis), shard.shape[dim])
        up = [(i, (i + 1) % devices) for i in range(devices)]
        down = [(j, i) for i, j in up]
        last = lax.slice_in_dim(shard, length - width, length, axis=dim)
        leading = lax.slice_in_dim(shard, 0, width, axis=dim)
        before = lax.ppermute(last, axis, up)
        after = lax.ppermute(leading, axis, down)
        shard = jnp.concatenate([before, shard, after], axis=dim)
    return shard


def from_behind(value, axis, steps):
    count = lax.axis_size(axis)
    pairs = [(source, (source + steps) % count) for source in range(count)]
    return lax.ppermute(value, axis, pairs)


def layer_norm(values):
    average = jnp.mean(values, axis=-1, keepdims=True)
    centred = values - average
    variance = jnp.mean(centred * centred, axis=-1, keepdims=True)
    inverse_dev = lax.rsqrt(variance + EPSILON)
    return (centred * inverse_dev, inverse_dev)


def norm_backward(grad_normed, standard, inverse_dev, norm_gain):
    grad_standard = grad_normed * norm_gain
    first_mean = jnp.mean(grad_standard, axis=-1, keepdims=True)
    second_mean = jnp.mean(grad_standard * standard, axis=-1, keepdims=True)
    return inverse_dev * (grad_standard - first_mean - standard * second_mean)


def attend_forward(queries, keys_values):
    query_count = queries.shape[0]
    key_count = keys_values.shape[0]
    score_scale = HEAD_DIM ** (-0.5)
    query_heads = queries.reshape(query_count, HEADS, HEAD_DIM)
    key_heads = keys_values[:, :INNER].reshape(key_count, HEADS, HEAD_DIM)
    value_heads = keys_values[:, INNER:].reshape(key_count, HEADS, HEAD_DIM)
    scores = (
        jnp.einsum("qhd,khd->hqk", query_heads, key_heads, preferred_element_type=jnp.float32)
        * score_scale
    )
    biggest = jnp.max(scores, axis=-1, keepdims=True)
    exponent = jnp.exp(scores - biggest)
    softmax_out = exponent / jnp.sum(exponent, axis=-1, keepdims=True)
    softmax_low = softmax_out.astype(jnp.bfloat16)
    attended = jnp.einsum(
        "hqk,khd->qhd", softmax_low, value_heads, preferred_element_type=jnp.float32
    )
    return (attended.astype(jnp.bfloat16).reshape(query_count, INNER), softmax_out)


def attend_backward(softmax_out, queries, keys_values, grad_attended):
    query_count = queries.shape[0]
    key_count = keys_values.shape[0]
    score_scale = HEAD_DIM ** (-0.5)
    query_heads = queries.reshape(query_count, HEADS, HEAD_DIM)
    key_heads = keys_values[:, :INNER].reshape(key_count, HEADS, HEAD_DIM)
    value_heads = keys_values[:, INNER:].reshape(key_count, HEADS, HEAD_DIM)
    grad_heads = grad_attended.reshape(query_count, HEADS, HEAD_DIM)
    softmax_low = softmax_out.astype(jnp.bfloat16)
    grad_values = jnp.einsum(
        "hqk,qhd->khd", softmax_low, grad_heads, preferred_element_type=jnp.float32
    )
    grad_weights = jnp.einsum(
        "qhd,khd->hqk", grad_heads, value_heads, preferred_element_type=jnp.float32
    )
    weighted = jnp.sum(softmax_out * grad_weights, axis=-1, keepdims=True)
    grad_scores = (softmax_out * (grad_weights - weighted)).astype(jnp.bfloat16)
    grad_queries = (
        jnp.einsum("hqk,khd->qhd", grad_scores, key_heads, preferred_element_type=jnp.float32)
        * score_scale
    )
    grad_keys = (
        jnp.einsum("hqk,qhd->khd", grad_scores, query_heads, preferred_element_type=jnp.float32)
        * score_scale
    )
    pair_gradient_rows = jnp.concatenate(
        [grad_keys.reshape(key_count, INNER), grad_values.reshape(key_count, INNER)], axis=1
    )
    return (grad_queries.astype(jnp.bfloat16).reshape(query_count, INNER), pair_gradient_rows)


def interp_weights(fine_index):
    coarse_cell = fine_index // 4
    phase_index = fine_index % 4
    lower_shift = (phase_index < 2).astype(jnp.int32)
    upper_weight = (2 * phase_index - 3 + 8 * lower_shift).astype(jnp.float32) / 8.0
    return (coarse_cell - lower_shift, upper_weight)


def build_matrix(lower_cell, upper_cell, upper_weight, count):
    columns = jnp.arange(count, dtype=jnp.int32)
    lower_part = jnp.where(
        columns[None, :] == lower_cell[:, None], 1.0 - upper_weight[:, None], 0.0
    )
    upper_portion = jnp.where(columns[None, :] == upper_cell[:, None], upper_weight[:, None], 0.0)
    return lower_part + upper_portion


def contract_last(left_side, right_side):
    return lax.dot_general(
        left_side, right_side, (((1,), (1,)), ((), ())), preferred_element_type=jnp.float32
    )


def shards(tokens, norm_gain, query_key_value_weight, out_weight, head_weight, coarse, grad_fine):
    lat_rows = tokens.shape[1]
    lon_cols = tokens.shape[2]
    row_count = lat_rows * lon_cols
    flattened_rows = tokens[0].reshape(row_count, D).astype(jnp.float32)
    standard, inverse_dev = layer_norm(flattened_rows)
    normed = (standard * norm_gain).astype(jnp.bfloat16)
    full_qkv = lax.all_gather(query_key_value_weight, "fsdp", axis=0, tiled=True)
    projected = jnp.dot(normed, full_qkv, preferred_element_type=jnp.float32).astype(jnp.bfloat16)
    queries = projected[:, :INNER]
    pairs_local = projected[:, INNER:]
    margin_pairs = with_halo(
        pairs_local.reshape(lat_rows, lon_cols, 2 * INNER), (("tile", 1),), MARGIN
    )
    keys_values = margin_pairs.reshape(lat_rows * (lon_cols + 2 * MARGIN), 2 * INNER)
    attended, softmax_out = attend_forward(queries, keys_values)
    full_out = lax.all_gather(out_weight, "fsdp", axis=0, tiled=True)
    mixed_out = jnp.dot(attended, full_out, preferred_element_type=jnp.float32)
    hidden = (flattened_rows + mixed_out).astype(jnp.bfloat16)
    full_head = lax.all_gather(head_weight, "fsdp", axis=0, tiled=True)
    head_out = jnp.dot(hidden, full_head, preferred_element_type=jnp.float32)
    fine_head = (
        head_out.reshape(lat_rows, lon_cols, VARS, 4, 4)
        .transpose(2, 0, 3, 1, 4)
        .reshape(VARS, 4 * lat_rows, 4 * lon_cols)
    )
    coarse_padded_grid = with_halo(coarse[0], (("tile", 2),), 1)
    lat_lower, lat_upper_weight = interp_weights(jnp.arange(4 * lat_rows, dtype=jnp.int32))
    latitude_matrix = build_matrix(
        jnp.clip(lat_lower, 0, lat_rows - 1),
        jnp.clip(lat_lower + 1, 0, lat_rows - 1),
        lat_upper_weight,
        lat_rows,
    )
    lon_lower, lon_upper_weight = interp_weights(jnp.arange(4 * lon_cols, dtype=jnp.int32))
    lon_matrix = build_matrix(lon_lower + 1, lon_lower + 2, lon_upper_weight, lon_cols + 2)
    incomplete_grid = jnp.einsum(
        "lj,kji->kli", latitude_matrix, coarse_padded_grid, precision=lax.Precision.HIGHEST
    )
    residual = jnp.einsum(
        "vrb,cb->vrc", incomplete_grid, lon_matrix, precision=lax.Precision.HIGHEST
    )
    fine_grid = fine_head + residual
    grad_rows = (
        grad_fine[0]
        .reshape(VARS, lat_rows, 4, lon_cols, 4)
        .transpose(1, 3, 0, 2, 4)
        .reshape(row_count, HEAD_OUT)
    )
    grad_rows = grad_rows.astype(jnp.bfloat16)
    head_term = lax.dot_general(
        hidden, grad_rows, (((0,), (0,)), ((), ())), preferred_element_type=jnp.float32
    )
    head_block = lax.psum_scatter(head_term, "fsdp", scatter_dimension=0, tiled=True)
    grad_head = lax.psum(head_block, ("dp", "tile"))
    grad_hidden = contract_last(grad_rows, full_head)
    grad_attended = contract_last(grad_hidden.astype(jnp.bfloat16), full_out).astype(jnp.bfloat16)
    grad_queries, pair_gradient_rows = attend_backward(
        softmax_out, queries, keys_values, grad_attended
    )
    pair_gradient_rows = pair_gradient_rows.reshape(lat_rows, lon_cols + 2 * MARGIN, 2 * INNER)
    from_left = from_behind(pair_gradient_rows[:, lon_cols + MARGIN :], "tile", 1)
    from_right = from_behind(pair_gradient_rows[:, :MARGIN], "tile", -1)
    own_cells = pair_gradient_rows[:, MARGIN : MARGIN + lon_cols]
    own_cells = own_cells + jnp.pad(from_left, ((0, 0), (0, lon_cols - MARGIN), (0, 0)))
    own_cells = own_cells + jnp.pad(from_right, ((0, 0), (lon_cols - MARGIN, 0), (0, 0)))
    grad_all = jnp.concatenate(
        [grad_queries, own_cells.reshape(row_count, 2 * INNER).astype(jnp.bfloat16)], axis=1
    )
    grad_normed = contract_last(grad_all, full_qkv)
    grad_input = grad_hidden + norm_backward(grad_normed, standard, inverse_dev, norm_gain)
    grad_tokens = grad_input.astype(jnp.bfloat16).reshape(1, lat_rows, lon_cols, D)
    return (fine_grid[None], grad_tokens, grad_head)


def solution(mesh):
    placed = (
        P(("dp", "fsdp"), None, "tile", None),
        P(),
        P("fsdp", None),
        P("fsdp", None),
        P("fsdp", None),
        P(("dp", "fsdp"), None, None, "tile"),
        P(("dp", "fsdp"), None, None, "tile"),
    )
    return jax.shard_map(
        shards,
        mesh=mesh,
        in_specs=placed,
        out_specs=(
            P(("dp", "fsdp"), None, None, "tile"),
            P(("dp", "fsdp"), None, "tile", None),
            P("fsdp", None),
        ),
        check_vma=False,
    )
```

profile of v0, /device:TPU:2, one launch (start us, length us, event | category | flops | bytes accessed | tf_op | source)
XLA Modules:
  0.0 943.6 jit_solution(4857148850893295786)
XLA Ops:
  10.4 3.4 collective-permute-start.2
  13.8 6.3 collective-permute-start.3
  25.7 46.6 %all_gather.11 = bf16[1536,320]{1,0:T(8,128)(2,1)S(1)} all-gather(bf16[96,320]{1,0:T(8,128)(2,1)} %param.11), channel_id=1, replica_groups=mesh['dp'=2,'fsdp'=16,'tile'=16] {'fsdp'}, dimensions={0}, use_global_device_ids=true | all-gather | bytes 1044480 | tf_op jit(solution)/shard_map/all_gather | solution.py:144
  75.7 2.1 convolution_bitcast_fusion.1
  77.8 55.1 %all-gather.3.cloned.1.call-done = bf16[1536,2304]{1,0:T(8,128)(2,1)} async-done(((bf16[96,2304]{1,0:T(8,128)(2,1)}), bf16[1536,2304]{1,0:T(8,128)(2,1)}) %all-gather.3.cloned.1.call-update) | async-done | bytes 7077904 | tf_op jit(solution)/shard_map/all_gather | solution.py:132
  132.9 5.3 convolution_convert_fusion
  140.0 3.2 collective-permute-start
  143.2 2.8 collective-permute-start.1
  146.0 86.6 %all-gather.5.cloned.1.call-done = bf16[768,1536]{1,0:T(8,128)(2,1)} async-done(((bf16[48,1536]{1,0:T(8,128)(2,1)}), bf16[768,1536]{1,0:T(8,128)(2,1)}) %all-gather.5.cloned.1.call-update) | async-done | bytes 2359312 | tf_op jit(solution)/shard_map/all_gather | solution.py:141
  232.6 3.2 convolution_convert_fusion.1
  235.8 1.9 copy.24
  237.8 1.8 slice.50
  239.6 1.9 copy.18
  243.9 2.1 copy.29
  246.1 2.1 copy.28
  248.2 4.0 fusion.57
  252.2 2.9 convolution_convert_fusion.2
  257.3 2.0 fusion.60
  260.7 3.0 copy.20
  263.8 3.0 copy.21
  266.8 2.6 convolution_bitcast_fusion
  271.0 2.7 concatenate.20
  274.9 3.0 multiply_reduce_fusion
  281.9 1.9 concatenate.19
  287.6 3.4 collective-permute-start.4
  291.1 2.8 collective-permute-start.5
  296.7 3.5 collective-permute-done.4
  300.2 3.3 collective-permute-done.5
  305.2 6.3 fusion.52
  311.6 73.0 %reduce-scatter.2.cloned.1.call-done = f32[96,320]{1,0:T(8,128)} async-done(((f32[1536,320]{1,0:T(8,128)}), f32[96,320]{1,0:T(8,128)}) %reduce-scatter.2.cloned.1.call-update) | async-done | bytes 122896 | tf_op jit(solution)/shard_map/reduce_scatter | solution.py:178
  384.5 2.9 add_convert_fusion
  387.4 548.1 %all-reduce.4.cloned.1.call-done = f32[96,320]{1,0:T(8,128)} async-done(((f32[96,320]{1,0:T(8,128)}), f32[96,320]{1,0:T(8,128)}) %all-reduce.4.cloned.1.call-update) | async-done | bytes 122896 | tf_op jit(solution)/shard_map/psum | solution.py:179
  (101 shorter events, 36.6 us)
Async XLA Ops:
  7.2 14.4 %copy-start = (bf16[1,8,32,1536]{3,2,1,0:T(8,128)(2,1)S(1)}, bf16[1,8,32,1536]{3,2,1,0:T(8,128)(2,1)}, u32[]{:S(2)}) copy-start(bf16[1,8,32,1536]{3,2,1,0:T(8,128)(2,1)} %param.7) | copy-start | bytes 2359300
  7.2 14.8 %copy-start.19 = (f32[1,20,32,128]{3,2,1,0:T(8,128)S(1)}, f32[1,20,32,128]{3,2,1,0:T(8,128)}, u32[]{:S(2)}) copy-start(f32[1,20,32,128]{3,2,1,0:T(8,128)} %param.13) | copy-start | bytes 983044
  7.2 125.7 %all-gather.3.cloned.1.call-start = ((), (), s32[]{:S(2)}) async-start(), calls=%async_computation.1 | async-start | bytes 7520256 | tf_op jit(solution)/shard_map/all_gather | solution.py:132
  7.9 224.7 %all-gather.5.cloned.1.call-start = ((), (), s32[]{:S(2)}) async-start(), calls=%async_computation.2 | async-start | bytes 2506752 | tf_op jit(solution)/shard_map/all_gather | solution.py:141
  8.7 375.8 %reduce-scatter.2.cloned.1.call-start = ((), (), s32[]{:S(2)}) async-start(), calls=%async_computation.3 | async-start | bytes 2506752 | tf_op jit(solution)/shard_map/reduce_scatter | solution.py:178
  10.4 65.2 %collective-permute-start.2 = (f32[20,8,1]{2,1,0:T(8,128)}, f32[20,8,1]{2,1,0:T(8,128)}, u32[]{:S(2)}, u32[]{:S(2)}) collective-permute-start(f32[20,8,1]{2,1,0:T(8,128)} %get-tuple-element.11), channel_id=1, source_target_pairs={{0,1},{1,2},{2,3},{3,4},{4,5},{5,6},{6,7},{7,8},{8,9},{9,10},{10,1... | collective-permute-start | bytes 1928 | tf_op jit(solution)/shard_map/ppermute | solution.py:23
  13.8 61.8 %collective-permute-start.3 = (f32[20,8,1]{2,1,0:T(8,128)}, f32[20,8,1]{2,1,0:T(8,128)}, u32[]{:S(2)}, u32[]{:S(2)}) collective-permute-start(f32[20,8,1]{2,1,0:T(8,128)} %get-tuple-element.12), channel_id=1, source_target_pairs={{1,0},{2,1},{3,2},{4,3},{5,4},{6,5},{7,6},{8,7},{9,8},{10,9},{11,1... | collective-permute-start | bytes 1928 | tf_op jit(solution)/shard_map/ppermute | solution.py:24
  72.3 1.6 copy-start.20
  72.3 3.4 copy-start.15
  138.2 1.8 copy-start.14
  140.0 101.5 %collective-permute-start = (bf16[8,8,1536]{2,1,0:T(8,128)(2,1)}, bf16[8,8,1536]{2,1,0:T(8,128)(2,1)}, u32[]{:S(2)}, u32[]{:S(2)}) collective-permute-start(bf16[8,8,1536]{2,1,0:T(8,128)(2,1)} %get-tuple-element.9), channel_id=1, source_target_pairs={{0,1},{1,2},{2,3},{3,4},{4,5},{5,6},{6,7},{7,8},{8,9},{9,10},{10,1... | collective-permute-start | bytes 589832 | tf_op jit(solution)/shard_map/ppermute | solution.py:23
  143.2 98.3 %collective-permute-start.1 = (bf16[8,8,1536]{2,1,0:T(8,128)(2,1)}, bf16[8,8,1536]{2,1,0:T(8,128)(2,1)}, u32[]{:S(2)}, u32[]{:S(2)}) collective-permute-start(bf16[8,8,1536]{2,1,0:T(8,128)(2,1)} %get-tuple-element.10), channel_id=1, source_target_pairs={{1,0},{2,1},{3,2},{4,3},{5,4},{6,5},{7,6},{8,7},{9,8},{10,9},{11,1... | collective-permute-start | bytes 589832 | tf_op jit(solution)/shard_map/ppermute | solution.py:24
  252.2 2.9 copy-start.4
  256.0 1.3 copy-start.10
  257.3 2.0 copy-start.12
  273.7 661.8 %all-reduce.4.cloned.1.call-start = ((), (), s32[]{:S(2)}) async-start(), calls=%async_computation.4 | async-start | bytes 294912 | tf_op jit(solution)/shard_map/psum | solution.py:179
  274.9 3.0 copy-start.3
  277.9 1.9 copy-start.9
  283.8 1.3 copy-start.8
  285.0 8.9 copy-start.2
  285.0 8.9 copy-start.6
  285.2 1.5 copy-start.5
  287.6 12.6 %collective-permute-start.4 = (f32[8,8,1536]{2,1,0:T(8,128)}, f32[8,8,1536]{2,1,0:T(8,128)}, u32[]{:S(2)}, u32[]{:S(2)}) collective-permute-start(f32[8,8,1536]{2,1,0:T(8,128)} %get-tuple-element.5), channel_id=1, source_target_pairs={{0,1},{1,2},{2,3},{3,4},{4,5},{5,6},{6,7},{7,8},{8,9},{9,10},{10,1... | collective-permute-start | bytes 1179656 | tf_op jit(solution)/shard_map/ppermute | solution.py:32
  291.0 4.5 copy-start.11
  291.0 4.5 copy-start.13
  291.0 4.5 copy-start.22
  291.0 4.5 copy-start.23
  291.0 4.5 copy-start.24
  291.1 4.5 copy-start.25
  291.1 12.4 %collective-permute-start.5 = (f32[8,8,1536]{2,1,0:T(8,128)}, f32[8,8,1536]{2,1,0:T(8,128)}, u32[]{:S(2)}, u32[]{:S(2)}) collective-permute-start(f32[8,8,1536]{2,1,0:T(8,128)} %get-tuple-element.6), channel_id=1, source_target_pairs={{0,15},{1,0},{2,1},{3,2},{4,3},{5,4},{6,5},{7,6},{8,7},{9,8},{10,9... | collective-permute-start | bytes 1179656 | tf_op jit(solution)/shard_map/ppermute | solution.py:32
  296.7 8.5 copy-start.18
  296.7 8.6 copy-start.21
  (4 other events, 4.4 us)
Sparse Core Ops, SparseCore 0:
  10.1 122.7 all-gather.2
  135.0 97.5 all-gather.4
  273.8 110.6 reduce-scatter.1
  387.3 548.2 all-reduce.3
where the time goes:
time: 945 us; the launch traced here: 944 us
  waiting for transfers between devices  771 us (82%)
  blocking collectives  46.6 us (5%)
  local copies, waits for them, and re-layouts  41.8 us (4%)
  matrix products  37.3 us (4%)
  starting transfers between devices  22.1 us (2%)
  between operations  14.2 us (2%)
  other arithmetic  10.8 us (1%)
    psum x1, waiting for transfers between devices, shards(): grad_head = lax.psum(head_block, ('dp', 'tile'))  548 us
    all_gather x1, waiting for transfers between devices, shards(): full_out = lax.all_gather(out_weight, 'fsdp', axis=0, tiled=True)  86.6 us
    reduce_scatter x1, waiting for transfers between devices, shards(): lax.psum_scatter(head_term, 'fsdp', scatter_dimension=0, tiled=True)  73 us
    all_gather x1, waiting for transfers between devices, shards(): lax.all_gather(query_key_value_weight, 'fsdp', axis=0, tiled=True)  55.1 us
    all_gather x1, blocking collectives, shards(): full_head = lax.all_gather(head_weight, 'fsdp', axis=0, tiled=True)  46.6 us
  transfers between devices with their start and end apart: 10, of which 6 were waited for; matrix products, arithmetic and copies ran while one was open for 5% of the time, Pallas kernels for 0%

commit v1 on v0

--- a/solution.py
+++ b/solution.py
@@ -176,7 +176,9 @@
         hidden, grad_rows, (((0,), (0,)), ((), ())), preferred_element_type=jnp.float32
     )
     head_block = lax.psum_scatter(head_term, "fsdp", scatter_dimension=0, tiled=True)
-    grad_head = lax.psum(head_block, ("dp", "tile"))
+    grad_head = head_block
+    for nth in ("dp", "tile"):
+        grad_head = lax.psum(grad_head, axis_name=nth)
     grad_hidden = contract_last(grad_rows, full_head)
     grad_attended = contract_last(grad_hidden.astype(jnp.bfloat16), full_out).astype(jnp.bfloat16)
     grad_queries, pair_gradient_rows = attend_backward(

time: 945 us -> 548 us (0.58)
  the two profiles are of different devices: /device:TPU:2 before, /device:TPU:32 now
where the time goes in v1:
time: 548 us; the launch traced here: 547 us
  waiting for transfers between devices  370 us (68%)
  local copies, waits for them, and re-layouts  43.4 us (8%)
  blocking collectives  41.2 us (8%)
  matrix products  39.1 us (7%)
  starting transfers between devices  27.8 us (5%)
  between operations  14.1 us (3%)
  other arithmetic  11.4 us (2%)
    psum x2, waiting for transfers between devices, shards(): grad_head = lax.psum(grad_head, axis_name=nth)  172 us
    all_gather x1, waiting for transfers between devices, shards(): full_out = lax.all_gather(out_weight, 'fsdp', axis=0, tiled=True)  83.2 us
    reduce_scatter x1, waiting for transfers between devices, shards(): lax.psum_scatter(head_term, 'fsdp', scatter_dimension=0, tiled=True)  56.7 us
    all_gather x1, waiting for transfers between devices, shards(): lax.all_gather(query_key_value_weight, 'fsdp', axis=0, tiled=True)  53.7 us
    all_gather x1, blocking collectives, shards(): full_head = lax.all_gather(head_weight, 'fsdp', axis=0, tiled=True)  41.2 us
    ppermute x2, starting transfers between devices, with_halo(): after = lax.ppermute(leading, axis, down)  12.4 us
    unnamed x58, local copies, waits for them, and re-layouts  12.2 us
    dot_general x3, matrix products, contract_last(): lax.dot_general(left_side, right_side, (((1,), (1,)), ((), ())), preferre...  11.7 us
  transfers between devices with their start and end apart: 11, of which 7 were waited for; matrix products, arithmetic and copies ran while one was open for 12% of the time, Pallas kernels for 0%

profile of v1, /device:TPU:32, one launch (start us, length us, event | category | flops | bytes accessed | tf_op | source)
XLA Modules:
  0.0 547.1 jit_solution(11208140094290061172)
XLA Ops:
  10.4 3.4 collective-permute-start.2
  13.8 5.8 %collective-permute-start.3 = (f32[20,8,1]{2,1,0:T(8,128)}, f32[20,8,1]{2,1,0:T(8,128)}, u32[]{:S(2)}, u32[]{:S(2)}) collective-permute-start(f32[20,8,1]{2,1,0:T(8,128)} %get-tuple-element.12), channel_id=1, source_target_pairs={{1,0},{2,1},{3,2},{4,3},{5,4},{6,5},{7,6},{8,7},{9,8},{10,9},{11,1... | collective-permute-start | bytes 1928 | tf_op jit(solution)/shard_map/ppermute | solution.py:24
  25.2 41.2 %all_gather.11 = bf16[1536,320]{1,0:T(8,128)(2,1)S(1)} all-gather(bf16[96,320]{1,0:T(8,128)(2,1)} %param.11), channel_id=1, replica_groups=mesh['dp'=2,'fsdp'=16,'tile'=16] {'fsdp'}, dimensions={0}, use_global_device_ids=true | all-gather | bytes 1044480 | tf_op jit(solution)/shard_map/all_gather | solution.py:144
  69.8 2.1 convolution_bitcast_fusion.1
  72.0 53.7 %all-gather.3.cloned.1.call-done = bf16[1536,2304]{1,0:T(8,128)(2,1)} async-done(((bf16[96,2304]{1,0:T(8,128)(2,1)}), bf16[1536,2304]{1,0:T(8,128)(2,1)}) %all-gather.3.cloned.1.call-update) | async-done | bytes 7077904 | tf_op jit(solution)/shard_map/all_gather | solution.py:132
  125.7 5.3 convolution_convert_fusion
  132.7 2.5 collective-permute-start
  135.3 6.6 %collective-permute-start.1 = (bf16[8,8,1536]{2,1,0:T(8,128)(2,1)}, bf16[8,8,1536]{2,1,0:T(8,128)(2,1)}, u32[]{:S(2)}, u32[]{:S(2)}) collective-permute-start(bf16[8,8,1536]{2,1,0:T(8,128)(2,1)} %get-tuple-element.10), channel_id=1, source_target_pairs={{1,0},{2,1},{3,2},{4,3},{5,4},{6,5},{7,6},{8,7},{9,8},{10,9},{11,1... | collective-permute-start | bytes 589832 | tf_op jit(solution)/shard_map/ppermute | solution.py:24
  141.9 83.2 %all-gather.5.cloned.1.call-done = bf16[768,1536]{1,0:T(8,128)(2,1)} async-done(((bf16[48,1536]{1,0:T(8,128)(2,1)}), bf16[768,1536]{1,0:T(8,128)(2,1)}) %all-gather.5.cloned.1.call-update) | async-done | bytes 2359312 | tf_op jit(solution)/shard_map/all_gather | solution.py:141
  225.1 3.3 convolution_convert_fusion.1
  228.4 1.9 copy.24
  232.1 1.9 copy.18
  236.5 2.1 copy.29
  238.6 2.2 copy.28
  240.8 4.0 fusion.57
  244.8 2.9 convolution_convert_fusion.2
  251.6 2.1 fusion.60
  253.9 2.4 fusion.58
  256.3 2.4 reshape.187
  258.7 3.1 copy.20
  261.8 3.1 copy.21
  266.5 2.8 concatenate.20
  269.3 3.0 multiply_reduce_fusion
  276.3 1.9 concatenate.19
  282.0 2.5 collective-permute-start.4
  284.5 6.7 %collective-permute-start.5 = (f32[8,8,1536]{2,1,0:T(8,128)}, f32[8,8,1536]{2,1,0:T(8,128)}, u32[]{:S(2)}, u32[]{:S(2)}) collective-permute-start(f32[8,8,1536]{2,1,0:T(8,128)} %get-tuple-element.6), channel_id=1, source_target_pairs={{0,15},{1,0},{2,1},{3,2},{4,3},{5,4},{6,5},{7,6},{8,7},{9,8},{10,9... | collective-permute-start | bytes 1179656 | tf_op jit(solution)/shard_map/ppermute | solution.py:32
  292.9 2.2 fusion.11
  299.6 6.9 %fusion.52 = (f32[256]{0:T(256)}, f32[256]{0:T(256)}, f32[256,1536]{1,0:T(8,128)}) fusion(f32[256]{0:T(256)S(1)} %rsqrt.12, f32[256]{0:T(256)S(1)} %div.51, bf16[1,8,32,1536]{3,2,1,0:T(8,128)(2,1)S(1)} %copy-done, f32[1536]{0:T(1024)S(1)} %copy-done.22, bf16[1536,2304]{1,0:T(8,128)(2,1)} %all-gather.3.cloned.1.call-done, ...), kind=kOutput, calls=%fused_computation.104 | convolution fusion | flops 1817050624 | bytes 10627072 | tf_op jit(solution)/shard_map/dot_general | solution.py:120
  306.5 56.7 %reduce-scatter.2.cloned.1.call-done = f32[96,320]{1,0:T(8,128)} async-done(((f32[1536,320]{1,0:T(8,128)}), f32[96,320]{1,0:T(8,128)}) %reduce-scatter.2.cloned.1.call-update) | async-done | bytes 122896 | tf_op jit(solution)/shard_map/reduce_scatter | solution.py:178
  364.0 62.1 %all-reduce.5.cloned.1.call-done = f32[96,320]{1,0:T(8,128)} async-done(((f32[96,320]{1,0:T(8,128)}), f32[96,320]{1,0:T(8,128)}) %all-reduce.5.cloned.1.call-update) | async-done | bytes 122896 | tf_op jit(solution)/shard_map/psum | solution.py:181
  426.0 2.9 add_convert_fusion
  428.9 110.1 %all-reduce.7.cloned.1.call-done = f32[96,320]{1,0:T(8,128)} async-done(((f32[96,320]{1,0:T(8,128)}), f32[96,320]{1,0:T(8,128)}) %all-reduce.7.cloned.1.call-update) | async-done | bytes 122896 | tf_op jit(solution)/shard_map/psum | solution.py:181
  (106 shorter events, 40.2 us)
Async XLA Ops:
  7.2 13.8 %copy-start = (bf16[1,8,32,1536]{3,2,1,0:T(8,128)(2,1)S(1)}, bf16[1,8,32,1536]{3,2,1,0:T(8,128)(2,1)}, u32[]{:S(2)}) copy-start(bf16[1,8,32,1536]{3,2,1,0:T(8,128)(2,1)} %param.7) | copy-start | bytes 2359300
  7.2 14.2 %copy-start.20 = (f32[1,20,32,128]{3,2,1,0:T(8,128)S(1)}, f32[1,20,32,128]{3,2,1,0:T(8,128)}, u32[]{:S(2)}) copy-start(f32[1,20,32,128]{3,2,1,0:T(8,128)} %param.13) | copy-start | bytes 983044
  7.2 118.5 %all-gather.3.cloned.1.call-start = ((), (), s32[]{:S(2)}) async-start(), calls=%async_computation.1 | async-start | bytes 7520256 | tf_op jit(solution)/shard_map/all_gather | solution.py:132
  7.9 217.2 %all-gather.5.cloned.1.call-start = ((), (), s32[]{:S(2)}) async-start(), calls=%async_computation.2 | async-start | bytes 2506752 | tf_op jit(solution)/shard_map/all_gather | solution.py:141
  8.7 354.5 %reduce-scatter.2.cloned.1.call-start = ((), (), s32[]{:S(2)}) async-start(), calls=%async_computation.3 | async-start | bytes 2506752 | tf_op jit(solution)/shard_map/reduce_scatter | solution.py:178
  10.4 59.4 %collective-permute-start.2 = (f32[20,8,1]{2,1,0:T(8,128)}, f32[20,8,1]{2,1,0:T(8,128)}, u32[]{:S(2)}, u32[]{:S(2)}) collective-permute-start(f32[20,8,1]{2,1,0:T(8,128)} %get-tuple-element.11), channel_id=1, source_target_pairs={{0,1},{1,2},{2,3},{3,4},{4,5},{5,6},{6,7},{7,8},{8,9},{9,10},{10,1... | collective-permute-start | bytes 1928 | tf_op jit(solution)/shard_map/ppermute | solution.py:23
  13.8 56.0 %collective-permute-start.3 = (f32[20,8,1]{2,1,0:T(8,128)}, f32[20,8,1]{2,1,0:T(8,128)}, u32[]{:S(2)}, u32[]{:S(2)}) collective-permute-start(f32[20,8,1]{2,1,0:T(8,128)} %get-tuple-element.12), channel_id=1, source_target_pairs={{1,0},{2,1},{3,2},{4,3},{5,4},{6,5},{7,6},{8,7},{9,8},{10,9},{11,1... | collective-permute-start | bytes 1928 | tf_op jit(solution)/shard_map/ppermute | solution.py:24
  66.4 3.4 copy-start.15
  130.9 1.8 copy-start.13
  132.7 101.3 %collective-permute-start = (bf16[8,8,1536]{2,1,0:T(8,128)(2,1)}, bf16[8,8,1536]{2,1,0:T(8,128)(2,1)}, u32[]{:S(2)}, u32[]{:S(2)}) collective-permute-start(bf16[8,8,1536]{2,1,0:T(8,128)(2,1)} %get-tuple-element.9), channel_id=1, source_target_pairs={{0,1},{1,2},{2,3},{3,4},{4,5},{5,6},{6,7},{7,8},{8,9},{9,10},{10,1... | collective-permute-start | bytes 589832 | tf_op jit(solution)/shard_map/ppermute | solution.py:23
  135.3 98.7 %collective-permute-start.1 = (bf16[8,8,1536]{2,1,0:T(8,128)(2,1)}, bf16[8,8,1536]{2,1,0:T(8,128)(2,1)}, u32[]{:S(2)}, u32[]{:S(2)}) collective-permute-start(bf16[8,8,1536]{2,1,0:T(8,128)(2,1)} %get-tuple-element.10), channel_id=1, source_target_pairs={{1,0},{2,1},{3,2},{4,3},{5,4},{6,5},{7,6},{8,7},{9,8},{10,9},{11,1... | collective-permute-start | bytes 589832 | tf_op jit(solution)/shard_map/ppermute | solution.py:24
  244.8 3.0 copy-start.3
  244.8 3.1 copy-start.17
  247.9 2.0 copy-start.5
  249.9 1.7 copy-start.12
  253.7 172.4 %all-reduce.5.cloned.1.call-start = ((), (), s32[]{:S(2)}) async-start(), calls=%async_computation.4 | async-start | bytes 294912 | tf_op jit(solution)/shard_map/psum | solution.py:181
  261.7 3.1 copy-start.14
  266.5 2.8 copy-start.16
  266.5 2.8 copy-start.18
  269.3 3.0 copy-start.4
  272.3 1.9 copy-start.11
  279.4 11.8 %copy-start.2 = (bf16[8,256,384]{2,1,0:T(8,128)(2,1)S(1)}, bf16[8,256,384]{2,1,0:T(8,128)(2,1)}, u32[]{:S(2)}) copy-start(bf16[8,256,384]{2,1,0:T(8,128)(2,1)} %copy-done.1) | copy-start | bytes 4718596
  279.4 11.8 %copy-start.8 = (bf16[384,768]{0,1:T(8,128)(2,1)S(1)}, bf16[384,768]{0,1:T(8,128)(2,1)}, u32[]{:S(2)}) copy-start(bf16[384,768]{0,1:T(8,128)(2,1)} %copy.29) | copy-start | bytes 1769476
  282.0 14.6 %collective-permute-start.4 = (f32[8,8,1536]{2,1,0:T(8,128)}, f32[8,8,1536]{2,1,0:T(8,128)}, u32[]{:S(2)}, u32[]{:S(2)}) collective-permute-start(f32[8,8,1536]{2,1,0:T(8,128)} %get-tuple-element.5), channel_id=1, source_target_pairs={{0,1},{1,2},{2,3},{3,4},{4,5},{5,6},{6,7},{7,8},{8,9},{9,10},{10,1... | collective-permute-start | bytes 1179656 | tf_op jit(solution)/shard_map/ppermute | solution.py:32
  284.5 8.4 %copy-start.23 = (s32[128]{0:T(128)S(1)}, s32[128]{0:T(128)}, u32[]{:S(2)}) copy-start(s32[128]{0:T(128)} %get-tuple-element.24) | copy-start | bytes 1540
  284.5 8.4 %copy-start.24 = (s32[128]{0:T(128)S(1)}, s32[128]{0:T(128)}, u32[]{:S(2)}) copy-start(s32[128]{0:T(128)} %get-tuple-element.25) | copy-start | bytes 1540
  284.5 8.4 %copy-start.25 = (f32[128]{0:T(128)S(1)}, f32[128]{0:T(128)}, u32[]{:S(2)}) copy-start(f32[128]{0:T(128)} %get-tuple-element.22) | copy-start | bytes 1540
  284.5 8.3 %copy-start.26 = (f32[128]{0:T(128)S(1)}, f32[128]{0:T(128)}, u32[]{:S(2)}) copy-start(f32[128]{0:T(128)} %get-tuple-element.23) | copy-start | bytes 1540
  284.5 13.3 %collective-permute-start.5 = (f32[8,8,1536]{2,1,0:T(8,128)}, f32[8,8,1536]{2,1,0:T(8,128)}, u32[]{:S(2)}, u32[]{:S(2)}) collective-permute-start(f32[8,8,1536]{2,1,0:T(8,128)} %get-tuple-element.6), channel_id=1, source_target_pairs={{0,15},{1,0},{2,1},{3,2},{4,3},{5,4},{6,5},{7,6},{8,7},{9,8},{10,9... | collective-permute-start | bytes 1179656 | tf_op jit(solution)/shard_map/ppermute | solution.py:32
  295.1 4.5 copy-start.19
  295.1 4.5 copy-start.22
  363.2 175.8 %all-reduce.7.cloned.1.call-start = ((), (), s32[]{:S(2)}) async-start(), calls=%async_computation.5 | async-start | bytes 294912 | tf_op jit(solution)/shard_map/psum | solution.py:181
  (6 other events, 7.3 us)
Sparse Core Ops, SparseCore 0:
  10.1 115.5 all-gather.2
  127.7 97.3 all-gather.4
  253.8 109.3 reduce-scatter.1
  365.9 60.0 all-reduce.4
  429.1 109.8 all-reduce.6
